TPU v7x, 256 devices: a whole 4x4x8 slice. The times are simulated.
256 devices in a mesh: tm: 8 (over z), lat: 32 (over y, x, core).
Axes of the slice: x: 4, y: 4, z: 8, core: 2. Of those that a mesh axis runs over, the one named last changes fastest.
Arguments:
- wind_east: bfloat16 [960, 256, 1440], P('tm', 'lat'), may hold values from -40 to 40
- wind_north: bfloat16 [960, 256, 1440], P('tm', 'lat'), may hold values from -40 to 40
- snap_counts: int32 [8], P('tm'), may hold values from 1 to 120, 320 in all
- snap_ids: int32 [960], P('tm'), may hold values from 0 to 8759
Outputs:
- basis: bfloat16 [32, 256, 1440], P(None, 'lat')
- coeffs: float32 [32, 960], P(None, 'tm')
Inputs may be any that keep to these rules, and one draw needn't show every extreme that they name: `snap_counts`: entry b counts the used slots of the b-th block of 120 slots, which are that block's first ones; the entries sum to 320 and one of them equals 120.
All inputs are finite; a program needn't handle non-finite values.
Results may differ from a plain program's by a relative error of at most 0.0072.
Values may be sent and summed in bfloat16 or wider, within the bound.
A program may use at most 64 MiB of HBM per device.

v0:
```python
import jax
import jax.numpy as jnp
from jax import lax
from jax.sharding import PartitionSpec as P

RANK = 32


def with_halo(cells, sides, width):
    for axis, dim in sides:
        count = lax.axis_size(axis)
        ends = count - 1
        head = lax.slice_in_dim(cells, 0, width, axis=dim)
        tail = lax.slice_in_dim(cells, cells.shape[dim] - width, cells.shape[dim], axis=dim)
        cells = jnp.concatenate(
            [
                lax.ppermute(tail, axis, [(i, (i + 1) % count) for i in range(ends)]),
                cells,
                lax.ppermute(head, axis, [((i + 1) % count, i) for i in range(ends)]),
            ],
            axis=dim,
        )
    return cells


def latitude_cosine(first_row, row_count, total_rows):
    row_index = first_row + jnp.arange(row_count, dtype=jnp.int32)
    return jnp.cos((total_rows // 2 - row_index).astype(jnp.float32) * (jnp.pi / 720.0))


def sign_table(snap_ids, rank_count):
    column = jnp.arange(rank_count, dtype=jnp.int32)
    mixed = snap_ids[:, None] * 1103515245 + column[None, :] * 40503 + 12345
    mixed = jnp.bitwise_xor(mixed, jnp.right_shift(mixed, 13))
    mixed = mixed * 1664525 + 1013904223
    mixed = jnp.bitwise_xor(mixed, jnp.right_shift(mixed, 16))
    flipped = jnp.bitwise_and(jnp.right_shift(mixed, 7), 1)
    return (1 - 2 * flipped).astype(jnp.bfloat16)


def metric_vorticity(padded_east, wind_north, padded_cosine, valid):
    scaled = padded_east.astype(jnp.float32) * padded_cosine[None, :, None]
    north_side = scaled[:, :-2]
    south_side = scaled[:, 2:]
    meridional = wind_north.astype(jnp.float32)
    zonal_diff = jnp.roll(meridional, -1, axis=2) - jnp.roll(meridional, 1, axis=2)
    weight = 0.5 / jnp.sqrt(padded_cosine[1:-1])
    field = (zonal_diff - north_side + south_side) * weight[None, :, None] * valid[:, None, None]
    return field.astype(jnp.bfloat16)


def local_gram(sketch, cell_total):
    return (
        lax.dot_general(
            sketch,
            sketch,
            (((1,), (1,)), ((), ())),
            precision=lax.Precision.HIGHEST,
            preferred_element_type=jnp.float32,
        )
        / cell_total
    )


def orthonormal(gram_sum, sketch):
    factor = jnp.linalg.cholesky(gram_sum)
    inverse = lax.linalg.triangular_solve(
        factor, jnp.eye(gram_sum.shape[0], dtype=jnp.float32), left_side=True, lower=True
    )
    return jnp.dot(
        inverse, sketch, precision=lax.Precision.HIGHEST, preferred_element_type=jnp.float32
    ).astype(jnp.bfloat16)


def local(wind_east, wind_north, snap_counts, snap_ids):
    snap_slots, band_rows, lon_count = wind_east.shape
    band_count = lax.axis_size("lat")
    first_row = lax.axis_index("lat") * band_rows - 1
    padded_cosine = latitude_cosine(first_row, band_rows + 2, band_rows * band_count)
    valid = (jnp.arange(snap_slots, dtype=jnp.int32) < snap_counts[0]).astype(jnp.float32)
    padded_east = with_halo(wind_east, (("lat", 1),), 1)
    field = metric_vorticity(padded_east, wind_north, padded_cosine, valid).reshape(
        snap_slots, band_rows * lon_count
    )
    signs_matrix = sign_table(snap_ids, RANK)
    sketch = jnp.dot(signs_matrix.T, field, preferred_element_type=jnp.float32)
    cell_total = band_rows * band_count * lon_count
    sketch = lax.psum(sketch, "tm")
    gram_sum = lax.psum(local_gram(sketch, cell_total), "lat")
    basis_flat = orthonormal(gram_sum, sketch)
    projected = (
        lax.dot_general(
            basis_flat, field, (((1,), (1,)), ((), ())), preferred_element_type=jnp.float32
        )
        / cell_total
    )
    coeffs = lax.psum(projected, "lat")
    return (basis_flat.reshape(basis_flat.shape[0], band_rows, lon_count), coeffs)


def solution(mesh):
    in_specs = (P("tm", "lat", None), P("tm", "lat", None), P("tm"), P("tm"))
    out_specs = (P(None, "lat", None), P(None, "tm"))
    return jax.shard_map(local, mesh=mesh, in_specs=in_specs, out_specs=out_specs, check_vma=False)
```

profile of v0, /device:TPU:32, one launch (start us, length us, event | category | flops | bytes accessed | tf_op | source)
XLA Modules:
  0.0 398.7 jit_solution(5653867448975015679)
XLA Ops:
  7.2 0.0 copy-start
  7.2 0.0 all-reduce.2.cloned.1.call-start
  7.2 4.0 %fusion.36 = (bf16[120,1,1440]{2,1,0:T(2,128)(2,1)S(1)}, bf16[120,1,1440]{2,1,0:T(2,128)(2,1)S(1)}) fusion(bf16[120,8,1440]{2,1,0:T(8,128)(2,1)} %param.4), kind=kLoop, calls=%fused_computation.55 | loop fusion | bytes 1382400 | tf_op jit(solution)/shard_map/slice | solution.py:14
  11.2 0.8 copy.21
  12.0 2.5 collective-permute-start
  14.5 0.8 copy.22
  15.3 1.3 collective-permute-start.1
  16.7 0.0 copy-done
  16.7 0.0 copy-start.3
  16.7 6.0 %fusion.35 = (f32[120,8,1439]{2,1,0:T(8,128)}, f32[120,8,1439]{2,1,0:T(8,128)}) fusion(bf16[120,8,1440]{2,1,0:T(8,128)(2,1)S(1)} %copy-done), kind=kLoop, calls=%fused_computation.54 | loop fusion | bytes 22103040 | tf_op jit(solution)/shard_map/jit(_roll_static)/slice | solution.py:46
  22.7 0.0 copy-start.1
  22.7 0.1 rsqrt_multiply_fusion
  23.6 0.0 copy-done.3
  23.6 0.9 fusion.34
  24.5 0.0 collective-permute-done
  24.5 1.6 copy.16
  26.0 0.0 collective-permute-done.1
  26.1 0.0 slice-start
  26.1 1.7 copy.17
  27.8 0.0 copy-done.1
  27.8 0.0 slice-start.1
  27.8 0.0 copy-start.2
  27.8 3.5 convert_multiply_fusion
  31.3 0.0 slice-done
  31.3 0.0 slice-done.1
  31.3 0.0 copy-done.2
  31.4 6.7 %fusion.2 = bf16[120,8,1440]{2,1,0:T(8,128)(2,1)} fusion(f32[120,10,1440]{2,1,0:T(8,128)S(1)} %convert_multiply_fusion, f32[120,8,1]{2,1,0:T(8,128)S(1)} %copy-done.2, f32[120,8,1439]{2,1,0:T(8,128)} %get-tuple-element.5, f32[120,8,1439]{2,1,0:T(8,128)S(1)} %bitcast.19, f32[120,8,1]{2,1,0:T(8,128)S(1)} %get-tuple-element.2, f32[120]{0:T(128)S(1)} %compare_convert_fusion, ...), kind=kLoop, calls=%fused_computation.5 | loop fusion | flops 11059200 | bytes 24883712 | tf_op jit(solution)/shard_map/convert_element_type | solution.py:49
  38.0 5.6 %reshape.40 = bf16[120,11520]{1,0:T(8,128)(2,1)S(1)} reshape(bf16[120,8,1440]{2,1,0:T(8,128)(2,1)} %fusion.2) | data formatting | bytes 5529600 | tf_op jit(solution)/shard_map/reshape | solution.py:82
  43.7 1.7 fusion.14
  45.4 0.0 all-reduce.2.cloned.1.call-update
  45.4 82.4 %all-reduce.2.cloned.1.call-done = f32[32,11520]{1,0:T(8,128)} async-done(((f32[32,11520]{1,0:T(8,128)}), f32[32,11520]{1,0:T(8,128)}) %all-reduce.2.cloned.1.call-update) | async-done | bytes 1474576 | tf_op jit(solution)/shard_map/psum | solution.py:88
  127.8 3.2 convolution_multiply_fusion.1
  131.0 124.3 %psum.22 = f32[32,32]{0,1:T(8,128)S(1)} all-reduce(f32[32,32]{0,1:T(8,128)S(1)} %convolution_multiply_fusion.1), channel_id=1, replica_groups=mesh['tm'=8,'lat'=32] {'lat'}, use_global_device_ids=true, to_apply=%region_1.2 | all-reduce | flops 1024 | bytes 8192 | tf_op jit(solution)/shard_map/psum | solution.py:89
  255.3 0.1 copy.19
  255.4 2.9 cholesky.17
  258.3 0.6 compare_reduce_fusion
  259.0 0.7 fusion.3
  259.6 2.4 custom-call.6
  262.1 0.2 fusion.11
  262.3 2.7 convolution_convert_fusion
  265.0 0.9 convolution_multiply_fusion
  266.0 2.1 reshape.41
  268.1 123.8 %psum.23 = f32[32,120]{1,0:T(8,128)} all-reduce(f32[32,120]{1,0:T(8,128)S(1)} %convolution_multiply_fusion), channel_id=1, replica_groups=mesh['tm'=8,'lat'=32] {'lat'}, use_global_device_ids=true, to_apply=%region_4.5 | all-reduce | flops 3840 | bytes 30720 | tf_op jit(solution)/shard_map/psum | solution.py:97
  (7 shorter events, 0.1 us)
Async XLA Ops:
  7.2 9.5 %copy-start = (bf16[120,8,1440]{2,1,0:T(8,128)(2,1)S(1)}, bf16[120,8,1440]{2,1,0:T(8,128)(2,1)}, u32[]{:S(2)}) copy-start(bf16[120,8,1440]{2,1,0:T(8,128)(2,1)} %param.5) | copy-start | bytes 8294404
  7.2 120.6 %all-reduce.2.cloned.1.call-start = ((), (), s32[]{:S(2)}) async-start(), calls=%async_computation | async-start | bytes 2949120 | tf_op jit(solution)/shard_map/psum | solution.py:88
  12.0 12.4 %collective-permute-start = (bf16[120,1,1440]{2,0,1:T(8,128)(2,1)}, bf16[120,1,1440]{2,0,1:T(8,128)(2,1)}, u32[]{:S(2)}, u32[]{:S(2)}) collective-permute-start(bf16[120,1,1440]{2,0,1:T(8,128)(2,1)} %copy.21), channel_id=1, source_target_pairs={{0,1},{1,2},{2,3},{3,4},{4,5},{5,6},{6,7},{7,8},{8,9},{9,10},{10,1... | collective-permute-start | bytes 1036808 | tf_op jit(solution)/shard_map/ppermute | solution.py:17
  15.3 10.7 %collective-permute-start.1 = (bf16[120,1,1440]{2,0,1:T(8,128)(2,1)}, bf16[120,1,1440]{2,0,1:T(8,128)(2,1)}, u32[]{:S(2)}, u32[]{:S(2)}) collective-permute-start(bf16[120,1,1440]{2,0,1:T(8,128)(2,1)} %copy.22), channel_id=1, source_target_pairs={{1,0},{2,1},{3,2},{4,3},{5,4},{6,5},{7,6},{8,7},{9,8},{10,9},{11,1... | collective-permute-start | bytes 1036808 | tf_op jit(solution)/shard_map/ppermute | solution.py:19
  16.7 6.9 %copy-start.3 = (s32[120]{0:T(128)S(1)}, s32[120]{0:T(128)}, u32[]{:S(2)}) copy-start(s32[120]{0:T(128)} %param.7) | copy-start | bytes 1444
  22.7 5.1 %copy-start.1 = (bf16[120,8,1440]{2,1,0:T(8,128)(2,1)S(1)}, bf16[120,8,1440]{2,1,0:T(8,128)(2,1)}, u32[]{:S(2)}) copy-start(bf16[120,8,1440]{2,1,0:T(8,128)(2,1)} %param.4) | copy-start | bytes 8294404
  26.1 5.3 %slice-start = ((s8[5898240]{0:T(1024)(128)(4,1)}), s8[4194304]{0:T(1024)(128)(4,1)S(1)}, s32[]{:S(2)}) async-start(s8[5898240]{0:T(1024)(128)(4,1)} %bitcast.18), calls=%async_computation.1 | async-start | bytes 8388608
  27.8 3.5 slice-start.1
  27.8 3.5 copy-start.2
Sparse Core Ops, SparseCore 0:
  45.5 82.2 all-reduce.1
where the time goes:
time: 399 us
  blocking collectives  248 us (62%)
  waiting for transfers between devices  82.5 us (21%)
  local copies, waits for them, and re-layouts  23.6 us (6%)
  other arithmetic  17 us (4%)
  between operations  15 us (4%)
  matrix products  8.73 us (2%)
    psum x1, blocking collectives, local(): gram_sum = lax.psum(local_gram(sketch, cell_total), 'lat')  124 us
    psum x1, blocking collectives, local(): coeffs = lax.psum(projected, 'lat')  124 us
    psum x1, waiting for transfers between devices, local(): sketch = lax.psum(sketch, 'tm')  82.4 us
  transfers between devices with their start and end apart: 3, of which 1 were waited for; matrix products, arithmetic and copies ran while one was open for 2% of the time, Pallas kernels for 0%

commit v1 on v0

--- a/solution.py
+++ b/solution.py
@@ -94,7 +94,10 @@
         )
         / cell_total
     )
-    coeffs = lax.psum(projected, "lat")
+    coeffs = projected
+    chips = lax.psum(1, "lat")
+    for to_i in [[(it, it ^ at) for it in range(chips)] for at in (1, 2, 4, 8, 16) if at < chips]:
+        coeffs = coeffs + lax.ppermute(coeffs, "lat", to_i)
     return (basis_flat.reshape(basis_flat.shape[0], band_rows, lon_count), coeffs)
 
 

time: 399 us -> 293 us (0.73)
  blocking collectives: 248 us -> 124 us
  waiting for transfers between devices: 82.5 us -> 99.5 us
    psum x1 -> x0, blocking collectives: 124 us -> none  [local(): coeffs = lax.psum(projected, 'lat')]
    ppermute x0 -> x5, waiting for transfers between devices: none -> 17.1 us  [local(): coeffs = coeffs + lax.ppermute(coeffs, 'lat', to_i)]
  transfers between devices with their start and end apart: 3 -> 8, of which waited for: 1 -> 6; matrix products, arithmetic and copies ran while one was open for 2% -> 4% of each run, Pallas kernels for 0% -> 0%
where the time goes in v1:
time: 293 us
  blocking collectives  124 us (42%)
  waiting for transfers between devices  99.5 us (34%)
  local copies, waits for them, and re-layouts  23.5 us (8%)
  other arithmetic  17.6 us (6%)
  between operations  15.1 us (5%)
  matrix products  8.72 us (3%)
  starting transfers between devices  3.91 us (1%)
    psum x1, blocking collectives, local(): gram_sum = lax.psum(local_gram(sketch, cell_total), 'lat')  124 us
    psum x1, waiting for transfers between devices, local(): sketch = lax.psum(sketch, 'tm')  82.4 us
    ppermute x5, waiting for transfers between devices, local(): coeffs = coeffs + lax.ppermute(coeffs, 'lat', to_i)  17.1 us
    slice x2, local copies, waits for them, and re-layouts, metric_vorticity(): jnp.roll(meridional, 1, axis=2)  6.83 us
    convert_element_type x1, other arithmetic, metric_vorticity(): return field.astype(jnp.bfloat16)  6.66 us
  transfers between devices with their start and end apart: 8, of which 6 were waited for; matrix products, arithmetic and copies ran while one was open for 4% of the time, Pallas kernels for 0%

profile of v1, /device:TPU:32, one launch (start us, length us, event | category | flops | bytes accessed | tf_op | source)
XLA Modules:
  0.0 292.6 jit_solution(8705762800760325848)
XLA Ops:
  7.2 0.0 copy-start
  7.2 0.0 all-reduce.2.cloned.1.call-start
  7.2 4.0 %fusion.36 = (bf16[120,1,1440]{2,1,0:T(2,128)(2,1)S(1)}, bf16[120,1,1440]{2,1,0:T(2,128)(2,1)S(1)}) fusion(bf16[120,8,1440]{2,1,0:T(8,128)(2,1)} %param.4), kind=kLoop, calls=%fused_computation.55 | loop fusion | bytes 1382400 | tf_op jit(solution)/shard_map/slice | solution.py:14
  11.2 0.8 copy.21
  12.0 2.5 collective-permute-start
  14.6 0.8 copy.22
  15.4 1.3 collective-permute-start.1
  16.7 0.0 copy-done
  16.7 0.0 copy-start.3
  16.7 6.0 %fusion.35 = (f32[120,8,1439]{2,1,0:T(8,128)}, f32[120,8,1439]{2,1,0:T(8,128)}) fusion(bf16[120,8,1440]{2,1,0:T(8,128)(2,1)S(1)} %copy-done), kind=kLoop, calls=%fused_computation.54 | loop fusion | bytes 22103040 | tf_op jit(solution)/shard_map/jit(_roll_static)/slice | solution.py:46
  22.7 0.0 copy-start.1
  22.7 0.1 rsqrt_multiply_fusion
  23.6 0.0 copy-done.3
  23.6 0.9 fusion.34
  24.5 0.0 collective-permute-done
  24.5 1.6 copy.16
  26.1 0.0 collective-permute-done.1
  26.1 0.0 slice-start
  26.1 1.7 copy.17
  27.8 0.0 copy-done.1
  27.8 0.0 slice-start.1
  27.8 0.0 copy-start.2
  27.8 3.5 %convert_multiply_fusion = f32[120,10,1440]{2,1,0:T(8,128)S(1)} fusion(bf16[120,1,1440]{2,1,0:T(2,128)(2,1)S(1)} %copy.17, bf16[120,8,1440]{2,1,0:T(8,128)(2,1)S(1)} %copy-done.1, bf16[120,1,1440]{2,1,0:T(2,128)(2,1)S(1)} %copy.16, f32[10]{0:T(128)S(1)} %multiply_cosine_fusion), kind=kLoop, calls=%fused_computation.1 | loop fusion | flops 12096000 | bytes 10368040 | tf_op jit(solution)/shard_map/mul | solution.py:42
  31.3 0.0 slice-done
  31.3 0.0 slice-done.1
  31.4 0.0 copy-done.2
  31.4 6.7 %fusion.2 = bf16[120,8,1440]{2,1,0:T(8,128)(2,1)} fusion(f32[120,10,1440]{2,1,0:T(8,128)S(1)} %convert_multiply_fusion, f32[120,8,1]{2,1,0:T(8,128)S(1)} %copy-done.2, f32[120,8,1439]{2,1,0:T(8,128)} %get-tuple-element.5, f32[120,8,1439]{2,1,0:T(8,128)S(1)} %bitcast.19, f32[120,8,1]{2,1,0:T(8,128)S(1)} %get-tuple-element.2, f32[120]{0:T(128)S(1)} %compare_convert_fusion, ...), kind=kLoop, calls=%fused_computation.5 | loop fusion | flops 11059200 | bytes 24883712 | tf_op jit(solution)/shard_map/convert_element_type | solution.py:49
  38.0 5.6 %reshape.40 = bf16[120,11520]{1,0:T(8,128)(2,1)S(1)} reshape(bf16[120,8,1440]{2,1,0:T(8,128)(2,1)} %fusion.2) | data formatting | bytes 5529600 | tf_op jit(solution)/shard_map/reshape | solution.py:82
  43.7 1.7 fusion.14
  45.4 0.0 all-reduce.2.cloned.1.call-update
  45.4 82.4 %all-reduce.2.cloned.1.call-done = f32[32,11520]{1,0:T(8,128)} async-done(((f32[32,11520]{1,0:T(8,128)}), f32[32,11520]{1,0:T(8,128)}) %all-reduce.2.cloned.1.call-update) | async-done | bytes 1474576 | tf_op jit(solution)/shard_map/psum | solution.py:88
  127.8 3.1 %convolution_multiply_fusion.1 = f32[32,32]{0,1:T(8,128)S(1)} fusion(f32[32,11520]{1,0:T(8,128)} %all-reduce.2.cloned.1.call-done), kind=kOutput, calls=%fused_computation.9 | convolution fusion | flops 141558784 | bytes 1478656 | tf_op jit(solution)/shard_map/dot_general | solution.py:54
  131.0 124.3 %psum.15 = f32[32,32]{0,1:T(8,128)S(1)} all-reduce(f32[32,32]{0,1:T(8,128)S(1)} %convolution_multiply_fusion.1), channel_id=1, replica_groups=mesh['tm'=8,'lat'=32] {'lat'}, use_global_device_ids=true, to_apply=%region_1.2 | all-reduce | flops 1024 | bytes 8192 | tf_op jit(solution)/shard_map/psum | solution.py:89
  255.3 0.1 copy.19
  255.4 2.9 cholesky.17
  258.3 0.6 compare_reduce_fusion
  259.0 0.7 fusion.3
  259.6 2.4 custom-call.6
  262.1 0.2 fusion.11
  262.3 2.7 convolution_convert_fusion
  265.0 0.9 convolution_multiply_fusion
  265.9 0.1 collective-permute-start.2
  266.0 1.2 collective-permute-done.2
  267.2 0.0 collective-permute-start.3
  267.2 3.7 %collective-permute-done.3 = f32[32,120]{1,0:T(8,128)S(1)} collective-permute-done((f32[32,120]{1,0:T(8,128)S(1)}, f32[32,120]{1,0:T(8,128)S(1)}, u32[]{:S(2)}, u32[]{:S(2)}) %collective-permute-start.3) | collective-permute-done | bytes 15392 | tf_op jit(solution)/shard_map/ppermute | solution.py:100
  270.9 0.0 collective-permute-start.4
  271.0 5.2 %collective-permute-done.4 = f32[32,120]{1,0:T(8,128)S(1)} collective-permute-done((f32[32,120]{1,0:T(8,128)S(1)}, f32[32,120]{1,0:T(8,128)S(1)}, u32[]{:S(2)}, u32[]{:S(2)}) %collective-permute-start.4) | collective-permute-done | bytes 15392 | tf_op jit(solution)/shard_map/ppermute | solution.py:100
  276.2 0.0 collective-permute-start.5
  276.2 3.7 %collective-permute-done.5 = f32[32,120]{1,0:T(8,128)S(1)} collective-permute-done((f32[32,120]{1,0:T(8,128)S(1)}, f32[32,120]{1,0:T(8,128)S(1)}, u32[]{:S(2)}, u32[]{:S(2)}) %collective-permute-start.5) | collective-permute-done | bytes 15392 | tf_op jit(solution)/shard_map/ppermute | solution.py:100
  279.9 0.0 collective-permute-start.6
  279.9 2.1 reshape.41
  282.0 3.2 %collective-permute-done.6 = f32[32,120]{1,0:T(8,128)S(1)} collective-permute-done((f32[32,120]{1,0:T(8,128)S(1)}, f32[32,120]{1,0:T(8,128)S(1)}, u32[]{:S(2)}, u32[]{:S(2)}) %collective-permute-start.6) | collective-permute-done | bytes 15392 | tf_op jit(solution)/shard_map/ppermute | solution.py:100
  285.2 0.6 add.84
  (11 shorter events, 0.1 us)
Async XLA Ops:
  7.2 9.6 %copy-start = (bf16[120,8,1440]{2,1,0:T(8,128)(2,1)S(1)}, bf16[120,8,1440]{2,1,0:T(8,128)(2,1)}, u32[]{:S(2)}) copy-start(bf16[120,8,1440]{2,1,0:T(8,128)(2,1)} %param.5) | copy-start | bytes 8294404
  7.2 120.6 %all-reduce.2.cloned.1.call-start = ((), (), s32[]{:S(2)}) async-start(), calls=%async_computation | async-start | bytes 2949120 | tf_op jit(solution)/shard_map/psum | solution.py:88
  12.0 12.4 %collective-permute-start = (bf16[120,1,1440]{2,0,1:T(8,128)(2,1)}, bf16[120,1,1440]{2,0,1:T(8,128)(2,1)}, u32[]{:S(2)}, u32[]{:S(2)}) collective-permute-start(bf16[120,1,1440]{2,0,1:T(8,128)(2,1)} %copy.21), channel_id=1, source_target_pairs={{0,1},{1,2},{2,3},{3,4},{4,5},{5,6},{6,7},{7,8},{8,9},{9,10},{10,1... | collective-permute-start | bytes 1036808 | tf_op jit(solution)/shard_map/ppermute | solution.py:17
  15.4 10.7 %collective-permute-start.1 = (bf16[120,1,1440]{2,0,1:T(8,128)(2,1)}, bf16[120,1,1440]{2,0,1:T(8,128)(2,1)}, u32[]{:S(2)}, u32[]{:S(2)}) collective-permute-start(bf16[120,1,1440]{2,0,1:T(8,128)(2,1)} %copy.22), channel_id=1, source_target_pairs={{1,0},{2,1},{3,2},{4,3},{5,4},{6,5},{7,6},{8,7},{9,8},{10,9},{11,1... | collective-permute-start | bytes 1036808 | tf_op jit(solution)/shard_map/ppermute | solution.py:19
  16.7 6.9 %copy-start.3 = (s32[120]{0:T(128)S(1)}, s32[120]{0:T(128)}, u32[]{:S(2)}) copy-start(s32[120]{0:T(128)} %param.7) | copy-start | bytes 1444
  22.7 5.1 %copy-start.1 = (bf16[120,8,1440]{2,1,0:T(8,128)(2,1)S(1)}, bf16[120,8,1440]{2,1,0:T(8,128)(2,1)}, u32[]{:S(2)}) copy-start(bf16[120,8,1440]{2,1,0:T(8,128)(2,1)} %param.4) | copy-start | bytes 8294404
  26.1 5.3 %slice-start = ((s8[5898240]{0:T(1024)(128)(4,1)}), s8[4194304]{0:T(1024)(128)(4,1)S(1)}, s32[]{:S(2)}) async-start(s8[5898240]{0:T(1024)(128)(4,1)} %bitcast.18), calls=%async_computation.1 | async-start | bytes 8388608
  27.8 3.5 %slice-start.1 = ((s8[5898240]{0:T(1024)(128)(4,1)}), s8[1703936]{0:T(1024)(128)(4,1)S(1)}, s32[]{:S(2)}) async-start(s8[5898240]{0:T(1024)(128)(4,1)} %bitcast.18), calls=%async_computation.2 | async-start | bytes 3407872
  27.8 3.5 %copy-start.2 = (f32[120,8,1]{2,1,0:T(8,128)S(1)}, f32[120,8,1]{2,1,0:T(8,128)}, u32[]{:S(2)}) copy-start(f32[120,8,1]{2,1,0:T(8,128)} %get-tuple-element.3) | copy-start | bytes 11524
  265.9 1.3 collective-permute-start.2
  267.2 3.7 %collective-permute-start.3 = (f32[32,120]{1,0:T(8,128)S(1)}, f32[32,120]{1,0:T(8,128)S(1)}, u32[]{:S(2)}, u32[]{:S(2)}) collective-permute-start(f32[32,120]{1,0:T(8,128)S(1)} %add.80), channel_id=1, source_target_pairs={{0,2},{1,3},{2,0},{3,1},{4,6},{5,7},{6,4},{7,5},{8,10},{9,11},{10,... | collective-permute-start | bytes 46088 | tf_op jit(solution)/shard_map/ppermute | solution.py:100
  270.9 5.2 %collective-permute-start.4 = (f32[32,120]{1,0:T(8,128)S(1)}, f32[32,120]{1,0:T(8,128)S(1)}, u32[]{:S(2)}, u32[]{:S(2)}) collective-permute-start(f32[32,120]{1,0:T(8,128)S(1)} %add.81), channel_id=1, source_target_pairs={{0,4},{1,5},{2,6},{3,7},{4,0},{5,1},{6,2},{7,3},{8,12},{9,13},{10,... | collective-permute-start | bytes 46088 | tf_op jit(solution)/shard_map/ppermute | solution.py:100
  276.2 3.7 %collective-permute-start.5 = (f32[32,120]{1,0:T(8,128)S(1)}, f32[32,120]{1,0:T(8,128)S(1)}, u32[]{:S(2)}, u32[]{:S(2)}) collective-permute-start(f32[32,120]{1,0:T(8,128)S(1)} %add.82), channel_id=1, source_target_pairs={{0,8},{1,9},{2,10},{3,11},{4,12},{5,13},{6,14},{7,15},{8,0},{9,1},... | collective-permute-start | bytes 46088 | tf_op jit(solution)/shard_map/ppermute | solution.py:100
  279.9 5.2 %collective-permute-start.6 = (f32[32,120]{1,0:T(8,128)S(1)}, f32[32,120]{1,0:T(8,128)S(1)}, u32[]{:S(2)}, u32[]{:S(2)}) collective-permute-start(f32[32,120]{1,0:T(8,128)S(1)} %add.83), channel_id=1, source_target_pairs={{0,16},{1,17},{2,18},{3,19},{4,20},{5,21},{6,22},{7,23},{8,24},{9,... | collective-permute-start | bytes 46088 | tf_op jit(solution)/shard_map/ppermute | solution.py:100
Sparse Core Ops, SparseCore 0:
  45.5 82.2 all-reduce.1
